TPU v7x, 32 devices: a whole 2x2x4 slice. The times are simulated.
32 devices in a mesh: groups: 2 (over x), seq: 16 (over z, y, core).
Axes of the slice: x: 2, y: 2, z: 4, core: 2. Of those that a mesh axis runs over, the one named last changes fastest.
Arguments:
- tokens: bfloat16 [8192, 4096], P(('groups', 'seq')), parts along dimension 0, may hold values from -14 to 14, as said below
- norm_gain: float32 [4096], replicated, may hold values from 0.25 to 1.75
- w_query: bfloat16 [4096, 2048], P('seq'), may hold values from -1 to 1, as said below
- w_key: bfloat16 [4096, 512], P('seq'), may hold values from -24 to 24
- w_value: bfloat16 [4096, 512], P('seq'), may hold values from -0.09375 to 0.09375
- passage_blocks: int32 [64], P(('groups', 'seq')), parts along dimension 0, may hold values from 0 to 9, as said below
Outputs:
- attended: bfloat16 [8192, 2048], P(('groups', 'seq')), parts along dimension 0
There are 2 independent parts, one for each index of `groups`. A program takes and returns all parts, laid end to end along the dimension named above; an argument that names none is the same for every part. Nothing has to cross between parts.
Inputs may be any that keep to these rules, and one draw needn't show every extreme that they name: `passage_blocks`: passage numbers never fall along the row; each passage covers 1 to 7 whole blocks; the first and the last passage of the row cover exactly 7. `tokens`: hidden states of order one. `w_query`: entries of order 4096 ** -0.5.
All inputs are finite; a program needn't handle non-finite values.
Results may differ from a plain program's by a relative error of at most 0.0049.
The roundings to bfloat16 on the way count: a program that leaves them out, or rounds other values in their place, can miss the bound.
Values may be sent and summed in bfloat16 or wider, within the bound.
A program may use at most 128 MiB of HBM per device.

v0:
```python
import functools
import math

import jax
import jax.numpy as jnp
from jax import lax
from jax.experimental import pallas as pl
from jax.experimental.pallas import tpu as pltpu
from jax.sharding import PartitionSpec as P

HD = 128
QH = 16
KVH = 4
REACH = 3
GQ = QH // KVH
MESH = pl.DeviceIdType.MESH
SETS = 2 + GQ
SW = 2 * HD
PIECES = 4
SLOTS = 2 * REACH + 4


def kernel(n_chips, tok_ref, gain_ref, wq_ref, wk_ref, wv_ref, id_ref, out_ref,
           xraw, xn, wkv, wq0, wq1, qbuf, win, idwin, obuf,
           send_sem, loc_sem, init_sem, zsem, xsem, tok_sem, id_sem, halo_sem, out_sem):
    nz = n_chips // 2
    rows, width = tok_ref.shape
    nblk = 2
    blk = rows // nblk
    g = lax.axis_index("groups")
    s = lax.axis_index("seq")
    gx = lax.rem(g, 2)
    gp = g + 1 - 2 * gx
    c = lax.rem(s, 2)
    p = s // 2
    y = lax.rem(p, 2)
    z = p // 2
    me4 = 2 * y + c
    sib4 = 2 * y + 1 - c
    ys4 = 2 * (1 - y) + c
    yo4 = 2 * (1 - y) + 1 - c

    sib = (g, 4 * z + sib4)
    ysame = (g, 4 * z + ys4)
    yother = (g, 4 * z + yo4)
    twin = (gp, s)
    zm, zp = (g, s - 4), (g, s + 4)
    has_zm, has_zp = z >= 1, z + 1 < nz

    sends = []
    counter = [0]

    def guarded(cond, f):
        if cond is None:
            f()
        else:
            pl.when(cond)(f)

    def send(src, dst, rsem, dev, cond=None):
        d = pltpu.make_async_remote_copy(src_ref=src, dst_ref=dst, send_sem=send_sem.at[counter[0]],
                                         recv_sem=rsem, device_id=dev, device_id_type=MESH)
        counter[0] += 1
        guarded(cond, d.start)
        sends.append((cond, d))

    def recv(dst, rsem, dev, cond=None):
        d = pltpu.make_async_remote_copy(src_ref=dst, dst_ref=dst, send_sem=send_sem.at[0],
                                         recv_sem=rsem, device_id=dev, device_id_type=MESH)
        guarded(cond, d.wait_recv)

    def local(src, dst, i):
        d = pltpu.make_async_copy(src, dst, loc_sem.at[i])
        d.start()
        return d

    bufs = (wkv, wq0, wq1)

    def columns(head, i):
        return pl.ds(pl.multiple_of(head * HD if i < 2 else head * (GQ * HD) + (i - 2) * HD, HD), HD)

    weights = (wk_ref, wv_ref) + (wq_ref,) * GQ
    places = tuple((bufs[i // 2], slice(i % 2 * HD, i % 2 * HD + HD)) for i in range(SETS))

    def unit(t, zz, half):
        buf, lanes = places[t]
        return buf.at[zz, :, :, half, :, lanes]

    def mates(t, half):
        buf, lanes = places[t]
        return buf.at[z, 1 - y, :, half, :, lanes]

    def full_part(i, head, yy, cc):
        buf, lanes = places[i]
        return weights[i].at[:, :, columns(head, i)], buf.at[z, yy, cc, :, :, lanes]

    def half_part(i, head, yy, cc):
        buf, lanes = places[i]
        return weights[i].at[gx, :, columns(head, i)], buf.at[z, yy, cc, gx, :, lanes]

    loc_w = [local(*full_part(i, me4, y, c), i) for i in range(SETS)]
    loc_x = local(tok_ref, xraw.at[me4], SETS)
    loc_id = local(id_ref, idwin.at[REACH + me4], SETS + 1)

    def blank(lo):
        def f():
            win[lo:lo + REACH] = jnp.zeros((REACH, rows, SW), jnp.bfloat16)
            idwin[lo:lo + REACH] = jnp.zeros((REACH,) + id_ref.shape, jnp.int32)
        return f

    pl.when(z < 1)(blank(0))
    pl.when(z + 1 >= nz)(blank(REACH + 4))

    barrier = pltpu.get_barrier_semaphore()
    for dev in (sib, ysame, yother, twin):
        pl.semaphore_signal(barrier, inc=1, device_id=dev, device_id_type=MESH)
    for cond, dev in ((has_zm, zm), (has_zp, zp)):
        guarded(cond, functools.partial(pl.semaphore_signal, barrier, inc=1, device_id=dev, device_id_type=MESH))
    pl.semaphore_wait(barrier, 4 + jnp.where(has_zm, 1, 0) + jnp.where(has_zp, 1, 0))

    prow = rows // PIECES
    for i in range(SETS):
        for k, (dev, head) in enumerate(((ysame, ys4), (yother, yo4))):
            a, b = half_part(i, head, y, c)
            send(a, b, init_sem.at[i, 1 + k], dev)
        a, b = full_part(i, sib4, y, c)
        send(a, b, init_sem.at[i, 0], sib)
    for i, dev in enumerate((sib, ysame, yother)):
        send(id_ref, idwin.at[REACH + me4], id_sem.at[i], dev)
    for j in range(PIECES):
        r = slice(j * prow, (j + 1) * prow)
        send(tok_ref.at[r], xraw.at[me4, r], tok_sem.at[0, j], ysame)
    send(tok_ref, xraw.at[me4], tok_sem.at[2, 0], sib)

    def relay(t, d):
        if d == 0:
            loc_w[t].wait()
            recv(full_part(t, me4, y, 1 - c)[1], init_sem.at[t, 0], sib)
            recv(half_part(t, me4, 1 - y, c)[1], init_sem.at[t, 1], ysame)
            recv(half_part(t, me4, 1 - y, 1 - c)[1], init_sem.at[t, 2], yother)
            own = unit(t, z, gx)
            send(own, own, zsem.at[t, 1, 1], zm, has_zm)
            send(own, own, zsem.at[t, 0, 1], zp, has_zp)
            send(mates(t, gx), mates(t, gx), xsem.at[t, 0, 0], twin)
            return
        left, right = unit(t, z - d, gx), unit(t, z + d, gx)
        has_l, has_r = z >= d, z + d < nz
        recv(right, zsem.at[t, 1, d], zp, has_r)
        if d + 1 < nz:
            send(right, right, zsem.at[t, 1, d + 1], zm, has_r & has_zm)
        recv(left, zsem.at[t, 0, d], zm, has_l)
        if d + 1 < nz:
            send(left, left, zsem.at[t, 0, d + 1], zp, has_l & has_zp)
        send(right, right, xsem.at[t, 1, d], twin, has_r)
        send(left, left, xsem.at[t, 0, d], twin, has_l)

    def finish(pair):
        for t in (2 * pair, 2 * pair + 1):
            recv(mates(t, 1 - gx), xsem.at[t, 0, 0], twin)
            for d in range(1, nz):
                recv(unit(t, z + d, 1 - gx), xsem.at[t, 1, d], twin, z + d < nz)
                recv(unit(t, z - d, 1 - gx), xsem.at[t, 0, d], twin, z >= d)

    def normalize(slot, first=0, count=None):
        step = 16
        count = rows if count is None else count

        def body(i, _):
            r = pl.ds(pl.multiple_of(first + i * step, step), step)
            wide = xraw[slot, r, :].astype(jnp.float32)
            inv = lax.rsqrt(jnp.mean(wide * wide, axis=-1, keepdims=True) + 1e-05)
            xn[slot, r, :] = (wide * inv * gain_ref[...]).astype(jnp.bfloat16)
            return 0

        lax.fori_loop(0, count // step, body, 0)

    def forward_tokens(j):
        r = slice(j * prow, (j + 1) * prow)
        recv(xraw.at[ys4, r], tok_sem.at[0, j], ysame)
        send(xraw.at[ys4, r], xraw.at[ys4, r], tok_sem.at[1, j], sib)
        normalize(ys4, j * prow, prow)

    def other_tokens(j):
        recv(xraw.at[yo4, j * prow:(j + 1) * prow], tok_sem.at[1, j], sib)
        normalize(yo4, j * prow, prow)

    def project_kv(yy):
        def body(ci, _):
            r = jnp.dot(xn[2 * yy + ci], wkv[...].reshape(width, SW), preferred_element_type=jnp.float32)
            win[REACH + 2 * yy + ci] = r.astype(jnp.bfloat16)
            return 0

        lax.fori_loop(0, 2, body, 0)

    def project_q(t, yy):
        buf = bufs[t]

        def body(i, _):
            i = 2 * yy + i
            r = jnp.dot(xn[i], buf[...].reshape(width, SW), preferred_element_type=jnp.float32).astype(jnp.bfloat16)
            qbuf[2 * (t - 1), i] = r[:, 0:HD]
            qbuf[2 * (t - 1) + 1, i] = r[:, HD:SW]
            return 0

        lax.fori_loop(0, 2, body, 0)

    def halo_send(yy, which):
        for slot in range(4):
            mine = (slot // 2) == yy
            a = win.at[REACH + slot]
            if slot > 0:
                send(a, win.at[slot - 1], halo_sem.at[0, slot - 1], zp, mine & has_zp)
            if slot < 3:
                send(a, win.at[REACH + 4 + slot], halo_sem.at[1, slot], zm, mine & has_zm)

    def halo_recv():
        for j in range(REACH):
            recv(win.at[j], halo_sem.at[0, j], zm, has_zm)
            recv(win.at[REACH + 4 + j], halo_sem.at[1, j], zp, has_zp)

    def ids_send():
        loc_id.wait()
        for i, (slot, dev) in enumerate(((sib4, sib), (ys4, ysame), (yo4, yother))):
            recv(idwin.at[REACH + slot], id_sem.at[i], dev)
        send(idwin.at[4:7], idwin.at[0:3], id_sem.at[3], zp, has_zp)
        send(idwin.at[3:6], idwin.at[7:10], id_sem.at[4], zm, has_zm)

    def ids_recv():
        recv(idwin.at[0:3], id_sem.at[3], zm, has_zm)
        recv(idwin.at[7:10], id_sem.at[4], zp, has_zp)

    rate = HD ** (-0.5) * math.log2(math.e)
    span = 2 * REACH + 1

    def attend(slot, t):
        key_ids = jnp.concatenate([idwin[slot + j, 0:1, :] for j in range(span)], axis=1)
        for qb in range(nblk):
            mine = idwin[REACH + slot, 0:1, qb * blk:qb * blk + HD]
            allowed = key_ids == jnp.concatenate([mine] * (span * rows // HD), axis=1)
            rr = slice(qb * blk, (qb + 1) * blk)

            def head(hh, _):
                q = qbuf[2 * t + hh, slot, rr, :]
                k = win[pl.ds(slot, span), :, 0:HD].reshape(span * rows, HD)
                v = win[pl.ds(slot, span), :, HD:SW].reshape(span * rows, HD)
                sc = lax.dot_general(q, k, (((1,), (1,)), ((), ())), preferred_element_type=jnp.float32)
                sc = jnp.where(allowed, sc, -1e30)
                top = jnp.max(sc, axis=-1, keepdims=True)
                w = jnp.exp2((sc - top) * rate)
                total = jnp.sum(w, axis=-1, keepdims=True)
                mixed = jnp.dot(w.astype(jnp.bfloat16), v, preferred_element_type=jnp.float32)
                obuf[t, slot, rr, pl.ds(pl.multiple_of(hh * HD, HD), HD)] = (mixed / total).astype(jnp.bfloat16)
                return 0

            lax.fori_loop(0, 2, head, 0)

    def out_cols(head, t):
        return out_ref.at[:, pl.ds(pl.multiple_of(head * (GQ * HD) + t * SW, HD), SW)]

    out_local = []

    def attend_set(t):
        for i, (slot, dev) in enumerate(((yo4, yother), (ys4, ysame), (sib4, sib), (me4, None))):
            attend(slot, t)
            src = obuf.at[t, slot]
            if dev is None:
                out_local.append(local(src, out_cols(me4, t), SETS + 2 + t))
            else:
                send(src, out_cols(me4, t), out_sem.at[t, i], dev)

    for t in range(SETS):
        relay(t, 0)
        if t == 2:
            loc_x.wait()
            normalize(me4)
    ids_send()
    for d in range(1, nz):
        for t in range(SETS):
            relay(t, d)
        if d == 1:
            recv(xraw.at[sib4], tok_sem.at[2, 0], sib)
            normalize(sib4)
            forward_tokens(0)
        if d == max(2, nz - 2):
            forward_tokens(1)
            other_tokens(0)
    finish(0)
    project_kv(y)
    halo_send(y, 0)
    forward_tokens(2)
    other_tokens(1)
    other_tokens(2)
    forward_tokens(3)
    other_tokens(3)
    project_kv(1 - y)
    halo_send(1 - y, 1)
    finish(1)
    project_q(1, y)
    project_q(1, 1 - y)
    ids_recv()
    halo_recv()
    attend_set(0)
    finish(2)
    project_q(2, y)
    project_q(2, 1 - y)
    attend_set(1)
    for t in range(2):
        for i, (dev, head) in enumerate(((yother, yo4), (ysame, ys4), (sib, sib4))):
            recv(out_cols(head, t), out_sem.at[t, i], dev)
    for d in out_local:
        d.wait()
    for cond, d in sends:
        guarded(cond, d.wait_send)


def solution(mesh):
    n_seq = mesh.shape["seq"]
    n_chips = n_seq // 2
    nz = n_chips // 2

    def on_device(tokens, norm_gain, w_query, w_key, w_value, passage_blocks):
        rows, width = tokens.shape
        ids = jnp.repeat(passage_blocks + 1, rows // passage_blocks.shape[0])
        ids = jnp.broadcast_to(ids[None, :], (8, rows))
        anywhere = pl.BlockSpec(memory_space=pl.ANY)
        vmem = pl.BlockSpec(memory_space=pltpu.VMEM)
        n_send = SETS * (4 * nz) + 3 * SETS + 3 + 2 * PIECES + 1 + 2 + 12 + 6 + 2
        bf = jnp.bfloat16
        dma = pltpu.SemaphoreType.DMA
        half = w_query.shape[0] // 2
        weight = pltpu.VMEM((nz, 2, 2, 2, half, SW), bf)
        halves = [w.reshape(2, half, w.shape[1]) for w in (w_query, w_key, w_value)]
        return pl.pallas_call(
            functools.partial(kernel, n_chips),
            out_shape=jax.ShapeDtypeStruct((rows, QH * HD), bf),
            in_specs=[anywhere, vmem, anywhere, anywhere, anywhere, anywhere],
            out_specs=anywhere,
            scratch_shapes=[
                pltpu.VMEM((4, rows, width), bf),
                pltpu.VMEM((4, rows, width), bf),
                weight, weight, weight,
                pltpu.VMEM((GQ, 4, rows, HD), bf),
                pltpu.VMEM((SLOTS, rows, SW), bf),
                pltpu.VMEM((SLOTS, 8, rows), jnp.int32),
                pltpu.VMEM((2, 4, rows, SW), bf),
                dma((n_send,)), dma((SETS + 4,)), dma((SETS, 3)), dma((SETS, 2, nz)), dma((SETS, 2, nz)),
                dma((3, PIECES)), dma((5,)), dma((2, REACH)), dma((2, 3)),
            ],
            compiler_params=pltpu.CompilerParams(
                collective_id=0, has_side_effects=True, vmem_limit_bytes=60 * 2**20),
        )(tokens, norm_gain[None, :], *halves, ids)

    in_specs = (
        P(("groups", "seq"), None),
        P(),
        P("seq", None),
        P("seq", None),
        P("seq", None),
        P(("groups", "seq")),
    )
    out_specs = P(("groups", "seq"), None)
    return jax.shard_map(on_device, mesh=mesh, in_specs=in_specs, out_specs=out_specs, check_vma=False)
```

profile of v0, /device:TPU:8, one launch (start us, length us, event | category | flops | bytes accessed | tf_op | source)
XLA Modules:
  0.0 108.4 jit_solution(9698167714141727629)
XLA Ops:
  0.0 0.7 broadcast_add_fusion
  0.7 0.1 broadcast_bitcast_fusion
  0.7 0.6 broadcast_in_dim.16.id_ref
  1.3 104.7 %shard_map.64 = bf16[256,2048]{1,0:T(8,128)(2,1)} custom-call(bf16[256,4096]{1,0:T(8,128)(2,1)} %tok_ref.1, f32[1,4096]{1,0:T(1,128)} %bitcast.9, bf16[2,128,2048]{2,1,0:T(8,128)(2,1)} %bitcast.6, bf16[2,128,512]{2,1,0:T(8,128)(2,1)} %bitcast.7, bf16[2,128,512]{2,1,0:T(8,128)(2,1)} %bitcast.8, s32[8,256]{1,0:T(8,128)} %broadcast_in_dim.16.id_ref), custom_call_target="tpu_custom_call" | custom-call | tf_op jit(solution)/shard_map/pallas_call | solution.py:332
  106.1 2.3 %copy.8 = bf16[256,2048]{1,0:T(8,128)(2,1)} copy(bf16[256,2048]{1,0:T(8,128)(2,1)} %shard_map.64) | data formatting | bytes 2097152
where the time goes:
time: 109 us; the launch traced here: 108 us
  Pallas kernels  105 us (96%)
  local copies, waits for them, and re-layouts  2.98 us (3%)
    pallas_call x1, Pallas kernels, on_device(): pl.pallas_call(functools.partial(kernel, n_chips), out_shape=jax.ShapeDty...  105 us
    unnamed x1, local copies, waits for them, and re-layouts  2.3 us

commit v1 on v0

v1 whole, which is shorter than its diff:
```python
import functools
import math

import jax
import jax.numpy as jnp
from jax import lax
from jax.experimental import pallas as pl
from jax.experimental.pallas import tpu as pltpu
from jax.sharding import PartitionSpec as P

HD = 128
QH = 16
KVH = 4
REACH = 3
GQ = QH // KVH
MESH = pl.DeviceIdType.MESH
SETS = 2 + GQ
SW = 2 * HD
PIECES = 4
SLOTS = 2 * REACH + 4
NCH = 2


def kernel(n_chips, tok_ref, gain_ref, wq_ref, wk_ref, wv_ref, id_ref, out_ref,
           xraw, xn, wkv, wq0, wq1, qbuf, win, onehot, idwin, obuf,
           send_sem, loc_sem, init_sem, zsem, xsem, tok_sem, id_sem, halo_sem, out_sem):
    nz = n_chips // 2
    rows, width = tok_ref.shape
    g = lax.axis_index("groups")
    s = lax.axis_index("seq")
    gx = lax.rem(g, 2)
    gp = g + 1 - 2 * gx
    c = lax.rem(s, 2)
    p = s // 2
    y = lax.rem(p, 2)
    z = p // 2
    me4 = 2 * y + c
    sib4 = 2 * y + 1 - c
    ys4 = 2 * (1 - y) + c
    yo4 = 2 * (1 - y) + 1 - c

    sib = (g, 4 * z + sib4)
    ysame = (g, 4 * z + ys4)
    yother = (g, 4 * z + yo4)
    twin = (gp, s)
    zm, zp = (g, s - 4), (g, s + 4)
    has_zm, has_zp = z >= 1, z + 1 < nz

    sends = []
    counter = [0]

    def guarded(cond, f):
        if cond is None:
            f()
        else:
            pl.when(cond)(f)

    def send(src, dst, rsem, dev, cond=None):
        d = pltpu.make_async_remote_copy(src_ref=src, dst_ref=dst, send_sem=send_sem.at[counter[0]],
                                         recv_sem=rsem, device_id=dev, device_id_type=MESH)
        counter[0] += 1
        guarded(cond, d.start)
        sends.append((cond, d))

    def recv(dst, rsem, dev, cond=None):
        d = pltpu.make_async_remote_copy(src_ref=dst, dst_ref=dst, send_sem=send_sem.at[0],
                                         recv_sem=rsem, device_id=dev, device_id_type=MESH)
        guarded(cond, d.wait_recv)

    def local(src, dst, i):
        d = pltpu.make_async_copy(src, dst, loc_sem.at[i])
        d.start()
        return d

    bufs = (wkv, wq0, wq1)

    def columns(head, i):
        return pl.ds(pl.multiple_of(head * HD if i < 2 else head * (GQ * HD) + (i - 2) * HD, HD), HD)

    weights = (wk_ref, wv_ref) + (wq_ref,) * GQ
    places = tuple((bufs[i // 2], slice(i % 2 * HD, i % 2 * HD + HD)) for i in range(SETS))

    def unit(t, zz, half):
        buf, lanes = places[t]
        return buf.at[zz, :, :, half, :, lanes]

    def mates(t, half):
        buf, lanes = places[t]
        return buf.at[z, 1 - y, :, half, :, lanes]

    def full_part(i, head, yy, cc):
        buf, lanes = places[i]
        return weights[i].at[:, :, columns(head, i)], buf.at[z, yy, cc, :, :, lanes]

    def half_part(i, head, yy, cc):
        buf, lanes = places[i]
        return weights[i].at[gx, :, columns(head, i)], buf.at[z, yy, cc, gx, :, lanes]

    loc_x = local(tok_ref, xraw.at[me4], SETS)
    loc_w = [local(*full_part(i, me4, y, c), i) for i in range(SETS)]

    barrier = pltpu.get_barrier_semaphore()
    for dev in (sib, ysame, yother, twin):
        pl.semaphore_signal(barrier, inc=1, device_id=dev, device_id_type=MESH)
    for cond, dev in ((has_zm, zm), (has_zp, zp)):
        guarded(cond, functools.partial(pl.semaphore_signal, barrier, inc=1, device_id=dev, device_id_type=MESH))

    first = lax.broadcasted_iota(jnp.int32, idwin.shape[1:], 0) == 0
    idwin[REACH + me4] = jnp.where(first, id_ref[0], id_ref[1]) + 1
    pl.semaphore_wait(barrier, 4 + jnp.where(has_zm, 1, 0) + jnp.where(has_zp, 1, 0))

    prow = rows // PIECES
    for i in range(SETS):
        for k, (dev, head) in enumerate(((ysame, ys4), (yother, yo4))):
            a, b = half_part(i, head, y, c)
            send(a, b, init_sem.at[i, 1 + k], dev)
        a, b = full_part(i, sib4, y, c)
        send(a, b, init_sem.at[i, 0], sib)
    for i, dev in enumerate((sib, ysame, yother)):
        own = idwin.at[REACH + me4]
        send(own, own, id_sem.at[i], dev)
    for j in range(PIECES):
        r = slice(j * prow, (j + 1) * prow)
        send(tok_ref.at[r], xraw.at[me4, r], tok_sem.at[0, j], ysame)
    send(tok_ref, xraw.at[me4], tok_sem.at[2, 0], sib)

    def blank(lo):
        def f():
            win[lo:lo + REACH] = jnp.zeros((REACH, rows, SW), jnp.bfloat16)
            idwin[lo:lo + REACH] = jnp.zeros((REACH,) + idwin.shape[1:], jnp.int32)
        return f

    def relay(t, d):
        if d == 0:
            loc_w[t].wait()
            recv(full_part(t, me4, y, 1 - c)[1], init_sem.at[t, 0], sib)
            recv(half_part(t, me4, 1 - y, c)[1], init_sem.at[t, 1], ysame)
            recv(half_part(t, me4, 1 - y, 1 - c)[1], init_sem.at[t, 2], yother)
            own = unit(t, z, gx)
            send(own, own, zsem.at[t, 1, 1], zm, has_zm)
            send(own, own, zsem.at[t, 0, 1], zp, has_zp)
            send(mates(t, gx), mates(t, gx), xsem.at[t, 0, 0], twin)
            return
        left, right = unit(t, z - d, gx), unit(t, z + d, gx)
        has_l, has_r = z >= d, z + d < nz
        recv(right, zsem.at[t, 1, d], zp, has_r)
        if d + 1 < nz:
            send(right, right, zsem.at[t, 1, d + 1], zm, has_r & has_zm)
        send(right, right, xsem.at[t, 1, d], twin, has_r)
        recv(left, zsem.at[t, 0, d], zm, has_l)
        if d + 1 < nz:
            send(left, left, zsem.at[t, 0, d + 1], zp, has_l & has_zp)
        send(left, left, xsem.at[t, 0, d], twin, has_l)

    def finish(pair):
        for t in (2 * pair, 2 * pair + 1):
            recv(mates(t, 1 - gx), xsem.at[t, 0, 0], twin)
            for d in range(1, nz):
                recv(unit(t, z + d, 1 - gx), xsem.at[t, 1, d], twin, z + d < nz)
                recv(unit(t, z - d, 1 - gx), xsem.at[t, 0, d], twin, z >= d)

    def normalize(slot, first=0, count=None):
        step = 16
        count = rows if count is None else count

        def body(i, _):
            r = pl.ds(pl.multiple_of(first + i * step, step), step)
            wide = xraw[slot, r, :].astype(jnp.float32)
            inv = lax.rsqrt(jnp.mean(wide * wide, axis=-1, keepdims=True) + 1e-05)
            xn[slot, r, :] = (wide * inv * gain_ref[...]).astype(jnp.bfloat16)
            return 0

        lax.fori_loop(0, count // step, body, 0)

    def tokens(j):
        r = slice(j * prow, (j + 1) * prow)
        recv(xraw.at[ys4, r], tok_sem.at[0, j], ysame)
        send(xraw.at[ys4, r], xraw.at[ys4, r], tok_sem.at[1, j], sib)
        normalize(ys4, j * prow, prow)
        recv(xraw.at[yo4, r], tok_sem.at[1, j], sib)
        normalize(yo4, j * prow, prow)

    def project(t, yy, ch):
        a = xn[pl.ds(2 * yy, 2), ch * HD:(ch + 1) * HD, :].reshape(2 * HD, width)
        r = jnp.dot(a, bufs[t][...].reshape(width, SW), preferred_element_type=jnp.float32).astype(jnp.bfloat16)
        for i in range(2):
            part = r[i * HD:(i + 1) * HD]
            if t == 0:
                win[REACH + 2 * yy + i, ch * HD:(ch + 1) * HD, :] = part
            else:
                for h in range(2):
                    qbuf[t - 1, 2 * yy + i, ch, h] = part[:, h * HD:(h + 1) * HD]

    def halo_send(yy, ch):
        r = slice(ch * HD, (ch + 1) * HD)
        for slot in range(4):
            mine = (slot // 2) == yy
            a = win.at[REACH + slot, r]
            if slot > 0:
                send(a, win.at[slot - 1, r], halo_sem.at[0, slot - 1, ch], zp, mine & has_zp)
            if slot < 3:
                send(a, win.at[REACH + 4 + slot, r], halo_sem.at[1, slot, ch], zm, mine & has_zm)

    def halo_recv():
        for j in range(REACH):
            for ch in range(NCH):
                r = slice(ch * HD, (ch + 1) * HD)
                recv(win.at[j, r], halo_sem.at[0, j, ch], zm, has_zm)
                recv(win.at[REACH + 4 + j, r], halo_sem.at[1, j, ch], zp, has_zp)

    def ids_send():
        for i, (slot, dev) in enumerate(((sib4, sib), (ys4, ysame), (yo4, yother))):
            recv(idwin.at[REACH + slot], id_sem.at[i], dev)
        send(idwin.at[4:7], idwin.at[0:3], id_sem.at[3], zp, has_zp)
        send(idwin.at[3:6], idwin.at[7:10], id_sem.at[4], zm, has_zm)

    def ids_recv():
        recv(idwin.at[0:3], id_sem.at[3], zm, has_zm)
        recv(idwin.at[7:10], id_sem.at[4], zp, has_zp)

    rate = HD ** (-0.5) * math.log2(math.e)
    span = (2 * REACH + 1) * NCH - 1

    def fill_onehot():
        def body(i, _):
            lane = lax.broadcasted_iota(jnp.int32, (HD, HD), 1)
            onehot[i] = jnp.where(lane == i, 1.0, 0.0).astype(jnp.bfloat16)
            return 0
        lax.fori_loop(0, SLOTS * NCH, body, 0)

    def attend(slot, t):
        lane = lax.broadcasted_iota(jnp.int32, (1, HD), 1)
        ids = jnp.zeros((1, HD), jnp.int32)
        for j in range(SLOTS * NCH):
            ids = jnp.where(lane == j, idwin[j // NCH, j % NCH:j % NCH + 1, :], ids)

        def body(qb, _):
            mine = idwin[REACH + slot, pl.ds(qb, 1), :]
            bias = jnp.where(ids == mine, 0.0, -1e30)
            bias = jnp.broadcast_to(bias, (2 * HD, HD)).astype(jnp.bfloat16)
            q = jnp.concatenate([qbuf[t, slot, qb].reshape(2 * HD, HD), bias], axis=1)
            at = pl.ds(NCH * slot + qb, span)
            kv = win.reshape(SLOTS * NCH, HD, SW)
            k = jnp.concatenate([kv[at, :, 0:HD].reshape(span * HD, HD),
                                 onehot[at].reshape(span * HD, HD)], axis=1)
            v = jnp.concatenate([kv[at, :, HD:SW].reshape(span * HD, HD),
                                 jnp.ones((span * HD, HD), jnp.bfloat16)], axis=1)
            sc = lax.dot_general(q, k, (((1,), (1,)), ((), ())), preferred_element_type=jnp.float32)
            top = jnp.max(sc, axis=-1, keepdims=True)
            w = jnp.exp2((sc - top) * rate).astype(jnp.bfloat16)
            o = jnp.dot(w, v, preferred_element_type=jnp.float32)
            o = (o[:, 0:HD] / o[:, HD:SW]).astype(jnp.bfloat16)
            rr = pl.ds(pl.multiple_of(qb * HD, HD), HD)
            obuf[t, slot, rr, 0:HD] = o[0:HD]
            obuf[t, slot, rr, HD:SW] = o[HD:SW]
            return 0

        lax.fori_loop(0, NCH, body, 0)

    def out_cols(head, t):
        return out_ref.at[:, pl.ds(pl.multiple_of(head * (GQ * HD) + t * SW, HD), SW)]

    out_local = []

    def attend_slots(t, group):
        for i, slot, dev in group:
            attend(slot, t)
            src = obuf.at[t, slot]
            if dev is None:
                out_local.append(local(src, out_cols(me4, t), SETS + 1 + t))
            else:
                send(src, out_cols(me4, t), out_sem.at[t, i], dev)

    order = sorted(((t, d) for t in range(SETS) for d in range(nz)),
                   key=lambda td: (nz - 1) * td[0] + (nz - 0.5) * td[1])
    after = {}

    def at_task(index, f):
        after.setdefault(min(index, len(order) - 1), []).append(f)

    def kv_early():
        finish(0)
        project(0, y, 0)
        project(0, y, 1)
        project(0, 1 - y, 0)

    def q_early():
        finish(1)
        project(1, y, 0)
        project(1, y, 1)
        project(1, 1 - y, 0)

    def own_tokens():
        loc_x.wait()
        normalize(me4)

    def sib_tokens():
        recv(xraw.at[sib4], tok_sem.at[2, 0], sib)
        normalize(sib4)
        fill_onehot()
        pl.when(z < 1)(blank(0))
        pl.when(z + 1 >= nz)(blank(REACH + 4))

    last = nz - 1
    at_task(order.index((2, 0)), own_tokens)
    at_task(order.index((3, 0)), ids_send)
    at_task(order.index((3, 0)), sib_tokens)
    at_task(order.index((0, last)), lambda: tokens(0))
    at_task(order.index((4, 1)), lambda: tokens(1))
    at_task(order.index((1, last)) + 2, kv_early)
    at_task(order.index((4, min(2, last))), lambda: tokens(2))
    at_task(order.index((3, last)) + 2, q_early)
    for i, (t, d) in enumerate(order):
        relay(t, d)
        for f in after.get(i, ()):
            f()
    halo_send(y, 0)
    halo_send(y, 1)
    halo_send(1 - y, 0)
    tokens(3)
    project(0, 1 - y, 1)
    halo_send(1 - y, 1)
    project(1, 1 - y, 1)
    finish(2)
    for yy in (1 - y, y):
        for ch in range(NCH):
            project(2, yy, ch)
    ids_recv()
    halo_recv()
    far = ((0, yo4, yother), (1, ys4, ysame))
    near = ((2, sib4, sib), (3, me4, None))
    attend_slots(0, far)
    attend_slots(1, far)
    attend_slots(0, near)
    attend_slots(1, near)
    for t in range(2):
        for i, (dev, head) in enumerate(((yother, yo4), (ysame, ys4), (sib, sib4))):
            recv(out_cols(head, t), out_sem.at[t, i], dev)
    for d in out_local:
        d.wait()
    for cond, d in sends:
        guarded(cond, d.wait_send)


def solution(mesh):
    n_seq = mesh.shape["seq"]
    n_chips = n_seq // 2
    nz = n_chips // 2

    def on_device(tokens, norm_gain, w_query, w_key, w_value, passage_blocks):
        rows, width = tokens.shape
        anywhere = pl.BlockSpec(memory_space=pl.ANY)
        vmem = pl.BlockSpec(memory_space=pltpu.VMEM)
        smem = pl.BlockSpec(memory_space=pltpu.SMEM)
        n_send = SETS * (4 * nz + 3) + 3 + 2 * PIECES + 1 + 2 + 12 * NCH + 6
        bf = jnp.bfloat16
        dma = pltpu.SemaphoreType.DMA
        half = w_query.shape[0] // 2
        weight = pltpu.VMEM((nz, 2, 2, 2, half, SW), bf)
        halves = [w.reshape(2, half, w.shape[1]) for w in (w_query, w_key, w_value)]
        return pl.pallas_call(
            functools.partial(kernel, n_chips),
            out_shape=jax.ShapeDtypeStruct((rows, QH * HD), bf),
            in_specs=[anywhere, vmem, anywhere, anywhere, anywhere, smem],
            out_specs=anywhere,
            scratch_shapes=[
                pltpu.VMEM((4, rows, width), bf),
                pltpu.VMEM((4, rows, width), bf),
                weight, weight, weight,
                pltpu.VMEM((2, 4, NCH, 2, HD, HD), bf),
                pltpu.VMEM((SLOTS, rows, SW), bf),
                pltpu.VMEM((SLOTS * NCH, HD, HD), bf),
                pltpu.VMEM((SLOTS, 8, HD), jnp.int32),
                pltpu.VMEM((2, 4, rows, SW), bf),
                dma((n_send,)), dma((SETS + 4,)), dma((SETS, 3)), dma((SETS, 2, nz)), dma((SETS, 2, nz)),
                dma((3, PIECES)), dma((5,)), dma((2, REACH, NCH)), dma((2, 3)),
            ],
            compiler_params=pltpu.CompilerParams(
                collective_id=0, has_side_effects=True, vmem_limit_bytes=60 * 2**20),
        )(tokens, norm_gain[None, :], *halves, passage_blocks)

    in_specs = (
        P(("groups", "seq"), None),
        P(),
        P("seq", None),
        P("seq", None),
        P("seq", None),
        P(("groups", "seq")),
    )
    out_specs = P(("groups", "seq"), None)
    return jax.shard_map(on_device, mesh=mesh, in_specs=in_specs, out_specs=out_specs, check_vma=False)
```

time: 109 us -> 102 us (0.936)
  the two profiles are of different devices: /device:TPU:8 before, /device:TPU:0 now
where the time goes in v1:
time: 102 us
  Pallas kernels  99.3 us (97%)
  local copies, waits for them, and re-layouts  2.3 us (2%)
    pallas_call x1, Pallas kernels, on_device(): pl.pallas_call(functools.partial(kernel, n_chips), out_shape=jax.ShapeDty...  99.3 us
    unnamed x1, local copies, waits for them, and re-layouts  2.3 us

profile of v1, /device:TPU:0, one launch (start us, length us, event | category | flops | bytes accessed | tf_op | source)
XLA Modules:
  0.0 101.6 jit_solution(14658604054973572761)
XLA Ops:
  0.0 99.3 %shard_map.64 = bf16[256,2048]{1,0:T(8,128)(2,1)} custom-call(bf16[256,4096]{1,0:T(8,128)(2,1)} %tok_ref.1, f32[1,4096]{1,0:T(1,128)} %bitcast.7, bf16[2,128,2048]{2,1,0:T(8,128)(2,1)} %bitcast.4, bf16[2,128,512]{2,1,0:T(8,128)(2,1)} %bitcast.5, bf16[2,128,512]{2,1,0:T(8,128)(2,1)} %bitcast.6, s32[2]{0:T(128)} %id_ref.1), custom_call_target="tpu_custom_call" | custom-call | tf_op jit(solution)/shard_map/pallas_call | solution.py:361
  99.3 2.3 %copy.8 = bf16[256,2048]{1,0:T(8,128)(2,1)} copy(bf16[256,2048]{1,0:T(8,128)(2,1)} %shard_map.64) | data formatting | bytes 2097152

commit v2 on v1

v2 whole, which is shorter than its diff:
```python
import functools
import math

import jax
import jax.numpy as jnp
from jax import lax
from jax.experimental import pallas as pl
from jax.experimental.pallas import tpu as pltpu
from jax.sharding import PartitionSpec as P

HD = 128
QH = 16
KVH = 4
REACH = 3
GQ = QH // KVH
MESH = pl.DeviceIdType.MESH
SETS = 2 + GQ
SW = 2 * HD
PIECES = 8
SLOTS = 2 * REACH + 4
NCH = 2


def kernel(n_chips, tok_ref, gain_ref, wq_ref, wk_ref, wv_ref, id_ref, out_ref,
           gain, ids_in, starts, xraw, xn, wk_in, wv_in, wq_in, wbuf, qbuf, win, idwin, obuf,
           send_sem, loc_sem, init_sem, zsem, xsem, tok_sem, id_sem, halo_sem, out_sem):
    nz = n_chips // 2
    rows, width = tok_ref.shape
    g = lax.axis_index("groups")
    s = lax.axis_index("seq")
    gx = lax.rem(g, 2)
    gp = g + 1 - 2 * gx
    c = lax.rem(s, 2)
    p = s // 2
    y = lax.rem(p, 2)
    z = p // 2
    me4 = 2 * y + c
    sib4 = 2 * y + 1 - c
    ys4 = 2 * (1 - y) + c
    yo4 = 2 * (1 - y) + 1 - c

    sib = (g, 4 * z + sib4)
    ysame = (g, 4 * z + ys4)
    yother = (g, 4 * z + yo4)
    twin = (gp, s)
    zm, zp = (g, s - 4), (g, s + 4)
    has_zm, has_zp = z >= 1, z + 1 < nz

    sends = []
    counter = [0]

    def guarded(cond, f):
        if cond is None:
            f()
        else:
            pl.when(cond)(f)

    def send(src, dst, rsem, dev, cond=None):
        d = pltpu.make_async_remote_copy(src_ref=src, dst_ref=dst, send_sem=send_sem.at[counter[0]],
                                         recv_sem=rsem, device_id=dev, device_id_type=MESH)
        counter[0] += 1
        guarded(cond, d.start)
        sends.append((cond, d))

    def recv(dst, rsem, dev, cond=None):
        d = pltpu.make_async_remote_copy(src_ref=dst, dst_ref=dst, send_sem=send_sem.at[0],
                                         recv_sem=rsem, device_id=dev, device_id_type=MESH)
        guarded(cond, d.wait_recv)

    def local(src, dst, i):
        d = pltpu.make_async_copy(src, dst, loc_sem.at[i])
        d.start()
        return d

    def columns(head, i):
        return pl.ds(pl.multiple_of(head * HD if i < 2 else head * (GQ * HD) + (i - 2) * HD, HD), HD)

    weights = (wk_in, wv_in) + (wq_in,) * GQ

    def unit(t, zz, half):
        return wbuf.at[t, half, zz]

    def mates(t, half):
        return wbuf.at[t, half, z, 1 - y]

    def full_part(i, head, yy, cc):
        return weights[i].at[:, :, columns(head, i)], wbuf.at[i, :, z, yy, cc]

    def half_part(i, head, yy, cc):
        return weights[i].at[gx, :, columns(head, i)], wbuf.at[i, gx, z, yy, cc]

    loc_in = [local(src, dst, SETS + 3 + i)
              for i, (src, dst) in enumerate(((wk_ref, wk_in), (wv_ref, wv_in), (wq_ref, wq_in),
                                              (id_ref, ids_in), (gain_ref, gain)))]

    barrier = pltpu.get_barrier_semaphore()
    for dev in (sib, ysame, yother, twin):
        pl.semaphore_signal(barrier, inc=1, device_id=dev, device_id_type=MESH)
    for cond, dev in ((has_zm, zm), (has_zp, zp)):
        guarded(cond, functools.partial(pl.semaphore_signal, barrier, inc=1, device_id=dev, device_id_type=MESH))

    loc_in[3].wait()
    for i in range(NCH):
        idwin[NCH * (REACH + me4) + i] = jnp.full(idwin.shape[1:], ids_in[i] + 1, jnp.int32)
    pl.semaphore_wait(barrier, 4 + jnp.where(has_zm, 1, 0) + jnp.where(has_zp, 1, 0))

    prow = rows // PIECES
    for i in range(SETS):
        if i < 3:
            loc_in[i].wait()
        for k, (dev, head) in enumerate(((ysame, ys4), (yother, yo4))):
            a, b = half_part(i, head, y, c)
            send(a, b, init_sem.at[i, 1 + k], dev)
        a, b = full_part(i, sib4, y, c)
        send(a, b, init_sem.at[i, 0], sib)
    loc_w = [local(*full_part(i, me4, y, c), i) for i in range(SETS)]
    loc_x = local(tok_ref, xraw.at[me4], SETS)
    for i, dev in enumerate((sib, ysame, yother)):
        own = idwin.at[pl.ds(NCH * (REACH + me4), NCH)]
        send(own, own, id_sem.at[i], dev)
    for j in range(PIECES):
        r = slice(j * prow, (j + 1) * prow)
        send(tok_ref.at[r], xraw.at[me4, r], tok_sem.at[0, j], ysame)
    send(tok_ref, xraw.at[me4], tok_sem.at[2, 0], sib)

    def blank(lo):
        def f():
            win[lo:lo + REACH] = jnp.zeros((REACH, rows, SW), jnp.bfloat16)
            idwin[NCH * lo:NCH * (lo + REACH)] = jnp.zeros((NCH * REACH,) + idwin.shape[1:], jnp.int32)
        return f

    def pieces(t):
        return 2 if t == 0 else 1

    def part(t, zz, half, k):
        ref = unit(t, zz, half)
        return ref if pieces(t) == 1 else ref.at[lax.rem(y + k, 2)]

    def gather(t):
        loc_w[t].wait()
        recv(full_part(t, me4, y, 1 - c)[1], init_sem.at[t, 0], sib)
        if pieces(t) == 2:
            relay_part(t, 0, 0)
        recv(half_part(t, me4, 1 - y, c)[1], init_sem.at[t, 1], ysame)
        recv(half_part(t, me4, 1 - y, 1 - c)[1], init_sem.at[t, 2], yother)
        send(mates(t, gx), mates(t, gx), xsem.at[t, 0, 0], twin)

    def relay_part(t, d, k):
        left, right = part(t, z - d, gx, k), part(t, z + d, gx, k)
        has_l, has_r = z >= d, z + d < nz
        if d == 0:
            send(left, left, zsem.at[t, 1, 1, k], zm, has_zm)
            send(left, left, zsem.at[t, 0, 1, k], zp, has_zp)
            return
        recv(right, zsem.at[t, 1, d, k], zp, has_r)
        if d + 1 < nz:
            send(right, right, zsem.at[t, 1, d + 1, k], zm, has_r & has_zm)
        recv(left, zsem.at[t, 0, d, k], zm, has_l)
        if d + 1 < nz:
            send(left, left, zsem.at[t, 0, d + 1, k], zp, has_l & has_zp)

    def relay(t, d):
        for k in range(pieces(t)):
            if d > 0 or k > 0 or pieces(t) == 1:
                relay_part(t, d, k)
        if d > 0:
            left, right = unit(t, z - d, gx), unit(t, z + d, gx)
            send(right, right, xsem.at[t, 1, d], twin, z + d < nz)
            send(left, left, xsem.at[t, 0, d], twin, z >= d)

    def finish(pair):
        for t in (2 * pair, 2 * pair + 1):
            recv(mates(t, 1 - gx), xsem.at[t, 0, 0], twin)
            for d in range(1, nz):
                recv(unit(t, z + d, 1 - gx), xsem.at[t, 1, d], twin, z + d < nz)
                recv(unit(t, z - d, 1 - gx), xsem.at[t, 0, d], twin, z >= d)

    def normalize(slot, first=0, count=None):
        step = 16
        count = rows if count is None else count

        def body(i, _):
            r = pl.ds(pl.multiple_of(first + i * step, step), step)
            wide = xraw[slot, r, :].astype(jnp.float32)
            inv = lax.rsqrt(jnp.mean(wide * wide, axis=-1, keepdims=True) + 1e-05)
            xn[slot, r, :] = (wide * inv * gain[...]).astype(jnp.bfloat16)
            return 0

        lax.fori_loop(0, count // step, body, 0)

    def tokens(start, stop):
        for j in range(start, stop):
            r = slice(j * prow, (j + 1) * prow)
            recv(xraw.at[ys4, r], tok_sem.at[0, j], ysame)
            send(xraw.at[ys4, r], xraw.at[ys4, r], tok_sem.at[1, j], sib)
            normalize(ys4, j * prow, prow)
        for j in range(start, stop):
            recv(xraw.at[yo4, j * prow:(j + 1) * prow], tok_sem.at[1, j], sib)
            normalize(yo4, j * prow, prow)

    def project(t, yy, ch):
        a = xn[pl.ds(2 * yy, 2), ch * HD:(ch + 1) * HD, :].reshape(2 * HD, width)
        w = jnp.concatenate(
            [jnp.concatenate([wbuf[2 * t + i, h, zz, yc // 2, yc % 2] for i in range(2)], axis=1)
             for zz in range(nz) for yc in range(4) for h in range(2)], axis=0)
        r = jnp.dot(a, w, preferred_element_type=jnp.float32).astype(jnp.bfloat16)
        for i in range(2):
            part = r[i * HD:(i + 1) * HD]
            if t == 0:
                win[REACH + 2 * yy + i, ch * HD:(ch + 1) * HD, :] = part
            else:
                for h in range(2):
                    qbuf[t - 1, 2 * yy + i, ch, h] = part[:, h * HD:(h + 1) * HD]

    def halo_send(yy, ch):
        r = slice(ch * HD, (ch + 1) * HD)
        for slot in range(4):
            mine = (slot // 2) == yy
            a = win.at[REACH + slot, r]
            if slot > 0:
                send(a, win.at[slot - 1, r], halo_sem.at[0, slot - 1, ch], zp, mine & has_zp)
            if slot < 3:
                send(a, win.at[REACH + 4 + slot, r], halo_sem.at[1, slot, ch], zm, mine & has_zm)

    def halo_recv():
        for j in range(REACH):
            for ch in range(NCH):
                r = slice(ch * HD, (ch + 1) * HD)
                recv(win.at[j, r], halo_sem.at[0, j, ch], zm, has_zm)
                recv(win.at[REACH + 4 + j, r], halo_sem.at[1, j, ch], zp, has_zp)

    def ids_send():
        for i, (slot, dev) in enumerate(((sib4, sib), (ys4, ysame), (yo4, yother))):
            recv(idwin.at[pl.ds(NCH * (REACH + slot), NCH)], id_sem.at[i], dev)
        edge = NCH * REACH
        a = NCH * (REACH + 4)
        send(idwin.at[a - edge:a], idwin.at[0:edge], id_sem.at[3], zp, has_zp)
        send(idwin.at[edge:2 * edge], idwin.at[a:a + edge], id_sem.at[4], zm, has_zm)

    def ids_recv():
        edge = NCH * REACH
        a = NCH * (REACH + 4)
        recv(idwin.at[0:edge], id_sem.at[3], zm, has_zm)
        recv(idwin.at[a:a + edge], id_sem.at[4], zp, has_zp)
        lane = lax.broadcasted_iota(jnp.int32, (8, HD), 1)
        ids = jnp.zeros((8, HD), jnp.int32)
        for j in range(SLOTS * NCH):
            ids = jnp.where(lane == j, idwin[j], ids)
        for j in range(edge, a):
            opening = jnp.min(jnp.where(ids == idwin[j], lane, j))
            starts[j - edge] = jnp.maximum(opening, j - edge)

    rate = HD ** (-0.5) * math.log2(math.e)
    span = REACH * NCH + 1

    def attend(slot, t):
        kv = win.reshape(SLOTS * NCH, HD, SW)
        for qb in range(NCH):
            mine = idwin[NCH * (REACH + slot) + qb, 0:1, :]
            start = starts[NCH * slot + qb]
            bias = jnp.concatenate(
                [jnp.where(idwin[start + j, 0:1, :] == mine, 0.0, -1e30) for j in range(span)], axis=1)
            q = qbuf[t, slot, qb].reshape(2 * HD, HD)
            at = pl.ds(start, span)
            k = kv[at, :, 0:HD].reshape(span * HD, HD)
            v = jnp.concatenate([kv[at, :, HD:SW].reshape(span * HD, HD),
                                 jnp.ones((span * HD, HD), jnp.bfloat16)], axis=1)
            sc = lax.dot_general(q, k, (((1,), (1,)), ((), ())), preferred_element_type=jnp.float32) + bias
            top = jnp.max(sc, axis=-1, keepdims=True)
            w = jnp.exp2((sc - top) * rate).astype(jnp.bfloat16)
            o = jnp.dot(w, v, preferred_element_type=jnp.float32)
            o = (o[:, 0:HD] / o[:, HD:SW]).astype(jnp.bfloat16)
            rr = slice(qb * HD, (qb + 1) * HD)
            obuf[t, slot, rr, 0:HD] = o[0:HD]
            obuf[t, slot, rr, HD:SW] = o[HD:SW]

    def out_cols(head, t):
        return out_ref.at[:, pl.ds(pl.multiple_of(head * (GQ * HD) + t * SW, HD), SW)]

    out_local = []

    def attend_slots(t, group):
        for i, slot, dev in group:
            attend(slot, t)
            src = obuf.at[t, slot]
            if dev is None:
                out_local.append(local(src, out_cols(me4, t), SETS + 1 + t))
            else:
                send(src, out_cols(me4, t), out_sem.at[t, i], dev)

    order = sorted(((t, d) for t in range(SETS) for d in range(nz)),
                   key=lambda td: (nz - 1) * td[0] + (nz - 0.5) * td[1])
    after = {}

    def at_task(index, f):
        after.setdefault(min(index, len(order) - 1), []).append(f)

    def kv_early():
        finish(0)
        project(0, y, 0)
        project(0, y, 1)
        halo_send(y, 0)
        halo_send(y, 1)
        project(0, 1 - y, 0)
        halo_send(1 - y, 0)

    def own_tokens():
        loc_x.wait()
        loc_in[4].wait()
        normalize(me4)

    def sib_tokens():
        recv(xraw.at[sib4], tok_sem.at[2, 0], sib)
        normalize(sib4)
        pl.when(z < 1)(blank(0))
        pl.when(z + 1 >= nz)(blank(REACH + 4))

    last = nz - 1
    at_task(order.index((2, 0)), own_tokens)
    at_task(order.index((3, 0)), ids_send)
    at_task(order.index((3, 0)), sib_tokens)
    at_task(order.index((0, last)), lambda: tokens(0, 2))
    at_task(order.index((4, 1)), lambda: tokens(2, 4))
    at_task(order.index((1, last)) + 2, kv_early)
    at_task(order.index((4, min(2, last))), lambda: tokens(4, 6))
    at_task(len(order) - 3, lambda: tokens(6, 7))
    gathered = 0
    for i, (t, d) in enumerate(order[:-1]):
        while gathered < SETS and (gathered <= t or d > 0 or gathered <= i + 1):
            gather(gathered)
            gathered += 1
        relay(t, d)
        for f in after.get(i, ()):
            f()
    tokens(7, 8)
    project(0, 1 - y, 1)
    halo_send(1 - y, 1)
    finish(1)
    project(1, 1 - y, 0)
    project(1, 1 - y, 1)
    relay(*order[-1])
    project(1, y, 0)
    project(1, y, 1)
    ids_recv()
    halo_recv()
    far = ((0, yo4, yother), (1, ys4, ysame))
    near = ((2, sib4, sib), (3, me4, None))
    attend_slots(0, far)
    attend_slots(0, near)
    finish(2)
    for yy in (1 - y, y):
        for ch in range(NCH):
            project(2, yy, ch)
    attend_slots(1, far)
    attend_slots(1, near)
    for t in range(2):
        for i, (dev, head) in enumerate(((yother, yo4), (ysame, ys4), (sib, sib4))):
            recv(out_cols(head, t), out_sem.at[t, i], dev)
    for d in out_local:
        d.wait()
    for cond, d in sends:
        guarded(cond, d.wait_send)


def solution(mesh):
    n_seq = mesh.shape["seq"]
    n_chips = n_seq // 2
    nz = n_chips // 2

    def on_device(tokens, norm_gain, w_query, w_key, w_value, passage_blocks):
        rows, width = tokens.shape
        anywhere = pl.BlockSpec(memory_space=pl.ANY)
        hbm = pl.BlockSpec(memory_space=pltpu.HBM)
        n_send = SETS * (4 * nz + 3) + 2 * nz + 3 + 2 * PIECES + 1 + 2 + 12 * NCH + 6
        bf = jnp.bfloat16
        dma = pltpu.SemaphoreType.DMA
        half = w_query.shape[0] // 2
        halves = [w.reshape(2, half, w.shape[1]) for w in (w_query, w_key, w_value)]
        return pl.pallas_call(
            functools.partial(kernel, n_chips),
            out_shape=jax.ShapeDtypeStruct((rows, QH * HD), bf),
            in_specs=[hbm] * 6,
            out_specs=anywhere,
            scratch_shapes=[
                pltpu.VMEM((1, width), jnp.float32),
                pltpu.SMEM(passage_blocks.shape, jnp.int32),
                pltpu.SMEM((4 * NCH,), jnp.int32),
                pltpu.VMEM((4, rows, width), bf),
                pltpu.VMEM((4, rows, width), bf),
                *(pltpu.VMEM((2, half, w.shape[1]), bf) for w in (w_key, w_value, w_query)),
                pltpu.VMEM((SETS, 2, nz, 2, 2, half, HD), bf),
                pltpu.VMEM((2, 4, NCH, 2, HD, HD), bf),
                pltpu.VMEM((SLOTS, rows, SW), bf),
                pltpu.VMEM((SLOTS * NCH, 8, HD), jnp.int32),
                pltpu.VMEM((2, 4, rows, SW), bf),
                dma((n_send,)), dma((SETS + 8,)), dma((SETS, 3)), dma((SETS, 2, nz, 2)), dma((SETS, 2, nz)),
                dma((3, PIECES)), dma((5,)), dma((2, REACH, NCH)), dma((2, 3)),
            ],
            compiler_params=pltpu.CompilerParams(
                collective_id=0, has_side_effects=True, vmem_limit_bytes=52 * 2**20),
        )(*(pltpu.with_memory_space_constraint(a, pltpu.HBM)
            for a in (tokens, norm_gain[None, :], *halves, passage_blocks)))

    in_specs = (
        P(("groups", "seq"), None),
        P(),
        P("seq", None),
        P("seq", None),
        P("seq", None),
        P(("groups", "seq")),
    )
    out_specs = P(("groups", "seq"), None)
    return jax.shard_map(on_device, mesh=mesh, in_specs=in_specs, out_specs=out_specs, check_vma=False)
```

time: 102 us -> 91.1 us (0.89)
  Pallas kernels: 99.3 us -> 89.4 us
  local copies, waits for them, and re-layouts: 2.3 us -> 0.97 us
    pallas_call x1, Pallas kernels: 99.3 us -> 89.4 us  [on_device(): pl.pallas_call(functools.partial(kernel, n_chips), out_shape=jax.ShapeDty...]
    unnamed x1, local copies, waits for them, and re-layouts: 2.3 us -> 0.97 us
where the time goes in v2:
time: 91.1 us; the launch traced here: 90.4 us
  Pallas kernels  89.4 us (98%)
  local copies, waits for them, and re-layouts  0.97 us (1%)
    pallas_call x1, Pallas kernels, on_device(): pl.pallas_call(functools.partial(kernel, n_chips), out_shape=jax.ShapeDty...  89.4 us

profile of v2, /device:TPU:0, one launch (start us, length us, event | category | flops | bytes accessed | tf_op | source)
XLA Modules:
  0.0 90.4 jit_solution(15260582591580968780)
XLA Ops:
  0.0 89.4 %shard_map.64 = bf16[256,2048]{1,0:T(8,128)(2,1)S(1)} custom-call(bf16[256,4096]{1,0:T(8,128)(2,1)} %tok_ref.1, f32[1,4096]{1,0:T(1,128)} %bitcast.7, bf16[2,128,2048]{2,1,0:T(8,128)(2,1)} %bitcast.4, bf16[2,128,512]{2,1,0:T(8,128)(2,1)} %bitcast.5, bf16[2,128,512]{2,1,0:T(8,128)(2,1)} %bitcast.6, s32[2]{0:T(128)} %id_ref.1), custom_call_target="tpu_custom_call" | custom-call | tf_op jit(solution)/shard_map/pallas_call | solution.py:379
  89.4 1.0 %copy.8 = bf16[256,2048]{1,0:T(8,128)(2,1)} copy(bf16[256,2048]{1,0:T(8,128)(2,1)S(1)} %shard_map.64) | data formatting | bytes 2097152

commit v3 on v2

v3 whole, which is shorter than its diff:
```python
import functools
import math

import jax
import jax.numpy as jnp
from jax import lax
from jax.experimental import pallas as pl
from jax.experimental.pallas import tpu as pltpu
from jax.sharding import PartitionSpec as P

HD = 128
QH = 16
KVH = 4
REACH = 3
GQ = QH // KVH
MESH = pl.DeviceIdType.MESH
SETS = 2 + GQ
SW = 2 * HD
PIECES = (0, 4, 8, 12, 14, 16)
SLOTS = 2 * REACH + 4
NCH = 2
LATE = (4, 5)
SPLIT = (2, 1, 1, 1, 1, 4)
CHUNKS = 3
(S_MATE, S_LATE, S_XMATE, S_SIB, S_IDS, S_IDUP, S_IDDOWN, S_TOK, S_UP, S_DOWN, S_OUT, S_X, S_Z) = range(13)


def kernel(n_chips, tok_ref, gain_ref, wq_ref, wk_ref, wv_ref, id_ref, out_ref,
           gain, ids_in, starts, xraw, xn, wk_in, wv_in, wq_in, wbuf, qbuf, win, idwin, obuf,
           send_sem, loc_sem, init_sem, late_sem, mate_sem, zsem, xsem, tok_sem, id_sem, halo_sem, out_sem):
    nz = n_chips // 2
    rows, width = tok_ref.shape
    g = lax.axis_index("groups")
    s = lax.axis_index("seq")
    gx = lax.rem(g, 2)
    gp = g + 1 - 2 * gx
    c = lax.rem(s, 2)
    p = s // 2
    y = lax.rem(p, 2)
    z = p // 2
    me4 = 2 * y + c
    sib4 = 2 * y + 1 - c
    ys4 = 2 * (1 - y) + c
    yo4 = 2 * (1 - y) + 1 - c

    sib = (g, 4 * z + sib4)
    ysame = (g, 4 * z + ys4)
    yother = (g, 4 * z + yo4)
    twin = (gp, s)
    zm, zp = (g, s - 4), (g, s + 4)
    has_zm, has_zp = z >= 1, z + 1 < nz

    def guarded(cond, f):
        if cond is None:
            f()
        else:
            pl.when(cond)(f)

    def send(group, src, dst, rsem, dev, cond=None):
        d = pltpu.make_async_remote_copy(src_ref=src, dst_ref=dst, send_sem=send_sem.at[group],
                                         recv_sem=rsem, device_id=dev, device_id_type=MESH)
        guarded(cond, d.start)

    def recv(dst, rsem, dev, cond=None):
        d = pltpu.make_async_remote_copy(src_ref=dst, dst_ref=dst, send_sem=send_sem.at[0],
                                         recv_sem=rsem, device_id=dev, device_id_type=MESH)
        guarded(cond, d.wait_recv)

    def sent(group, like, cond=None):
        d = pltpu.make_async_remote_copy(src_ref=like, dst_ref=like, send_sem=send_sem.at[group],
                                         recv_sem=init_sem.at[0], device_id=sib, device_id_type=MESH)
        guarded(cond, d.wait_send)

    def local(src, dst, i):
        d = pltpu.make_async_copy(src, dst, loc_sem.at[i])
        d.start()
        return d

    def columns(head, i):
        return pl.ds(pl.multiple_of(head * HD if i < 2 else head * (GQ * HD) + (i - 2) * HD, HD), HD)

    weights = (wk_in, wv_in) + (wq_in,) * GQ

    def unit(t, zz, half):
        return wbuf.at[t, half, zz]

    def mates(t, half):
        return wbuf.at[t, half, z, 1 - y]

    def full_part(i, head, yy, cc):
        return weights[i].at[:, :, columns(head, i)], wbuf.at[i, :, z, yy, cc]

    def half_part(i, head, yy, cc, half):
        return weights[i].at[half, :, columns(head, i)], wbuf.at[i, half, z, yy, cc]

    loc_in = [local(src, dst, 3 + i)
              for i, (src, dst) in enumerate(((wk_ref, wk_in), (wv_ref, wv_in), (wq_ref, wq_in),
                                              (id_ref, ids_in), (gain_ref, gain)))]

    barrier = pltpu.get_barrier_semaphore()
    for dev in (sib, ysame, yother, twin):
        pl.semaphore_signal(barrier, inc=1, device_id=dev, device_id_type=MESH)
    for cond, dev in ((has_zm, zm), (has_zp, zp)):
        guarded(cond, functools.partial(pl.semaphore_signal, barrier, inc=1, device_id=dev, device_id_type=MESH))

    loc_in[3].wait()
    for i in range(NCH):
        idwin[NCH * (REACH + me4) + i] = jnp.full(idwin.shape[1:], ids_in[i] + 1, jnp.int32)
    pl.semaphore_wait(barrier, 4 + jnp.where(has_zm, 1, 0) + jnp.where(has_zp, 1, 0))

    pcuts = [rows * q // 16 for q in PIECES]
    cuts = (0, rows // 2, rows // 4 * 3, rows)
    for i in range(SETS):
        if i < 3:
            loc_in[i].wait()
        for dev, head in ((ysame, ys4), (yother, yo4)):
            a, b = half_part(i, head, y, c, gx)
            send(S_MATE, a, b, init_sem.at[1 + i], dev)
        a, b = full_part(i, sib4, y, c)
        send(S_SIB, a, b, init_sem.at[0 if SPLIT[i] == 2 else 1 + i], sib)
    for i in range(SETS):
        local(*full_part(i, me4, y, c), 0)
    loc_x = local(tok_ref, xraw.at[me4], 1)
    own_ids = idwin.at[pl.ds(NCH * (REACH + me4), NCH)]
    for dev in (sib, ysame, yother):
        send(S_IDS, own_ids, own_ids, id_sem.at[0], dev)
    for j in range(len(PIECES) - 1):
        r = slice(*pcuts[j:j + 2])
        send(S_TOK, tok_ref.at[r], xraw.at[me4, r], tok_sem.at[0, j], ysame)
    for i in LATE:
        for dev, head in ((ysame, ys4), (yother, yo4)):
            a, b = half_part(i, head, y, c, 1 - gx)
            send(S_LATE, a, b, late_sem, dev)
    send(S_TOK, tok_ref, xraw.at[me4], tok_sem.at[2, 0], sib)

    def blank(lo):
        def f():
            win[lo:lo + REACH] = jnp.zeros((REACH, rows, SW), jnp.bfloat16)
            idwin[NCH * lo:NCH * (lo + REACH)] = jnp.zeros((NCH * REACH,) + idwin.shape[1:], jnp.int32)
        return f

    def parts(t, zz, half):
        ref = unit(t, zz, half)
        if SPLIT[t] == 4:
            return [ref.at[k // 2, k % 2] for k in range(4)]
        if SPLIT[t] == 2:
            return [ref.at[y], ref.at[1 - y]]
        return [ref]

    zkeys = {}

    def z_at(*key):
        return zsem.at[zkeys.setdefault(key, len(zkeys))]

    def gather(t):
        if t == 0:
            like = wbuf.at[:, :, 0, 0, 0]
            pltpu.make_async_copy(like, like, loc_sem.at[0]).wait()
        if SPLIT[t] == 2:
            recv(full_part(t, me4, y, 1 - c)[1], init_sem.at[0], sib)
            relay_part(t, 0, 0)
            recv(wbuf.at[t, gx, z, 1 - y], init_sem.at[1 + t], ysame)
        else:
            recv(wbuf.at[t, gx, z], init_sem.at[1 + t], ysame)
        if t not in LATE:
            send(S_XMATE, mates(t, gx), mates(t, gx), mate_sem.at[t // 2], twin)

    def relay_part(t, d, k):
        for way, (zz, has, back, has_on, on) in enumerate((
                (z - d, z >= d, zm, has_zp, zp), (z + d, z + d < nz, zp, has_zm, zm))):
            ref = parts(t, zz, gx)[k]
            if d > 0:
                recv(ref, z_at(t, way, d, k), back, has)
            if d + 1 < nz:
                send(S_Z + 2 * d + way, ref, ref, z_at(t, way, d + 1, k), on, has & has_on if d > 0 else has_on)
            if d > 0:
                send(S_X, ref, ref, xsem.at[t // 2], twin, has)

    def relay(t, d):
        for k in range(SPLIT[t]):
            if d > 0 or k > 0 or SPLIT[t] != 2:
                relay_part(t, d, k)

    def finish(pair):
        if 2 * pair in LATE:
            recv(wbuf.at[2 * pair:2 * pair + 2, 1 - gx, z, 1 - y], late_sem, ysame)
        else:
            recv(wbuf.at[2 * pair:2 * pair + 2, 1 - gx, z, 1 - y], mate_sem.at[pair], twin)
        recv(wbuf.at[2 * pair:2 * pair + 2, 1 - gx, 0:nz - 1], xsem.at[pair], twin)

    def normalize(slot, first=0, count=None):
        step = 16
        count = rows if count is None else count

        def body(i, _):
            r = pl.ds(pl.multiple_of(first + i * step, step), step)
            wide = xraw[slot, r, :].astype(jnp.float32)
            inv = lax.rsqrt(jnp.mean(wide * wide, axis=-1, keepdims=True) + 1e-05)
            xn[slot, r, :] = (wide * inv * gain[...]).astype(jnp.bfloat16)
            return 0

        lax.fori_loop(0, count // step, body, 0)

    def tokens(j):
        r = slice(*pcuts[j:j + 2])
        recv(xraw.at[ys4, r], tok_sem.at[0, j], ysame)
        send(S_TOK, xraw.at[ys4, r], xraw.at[ys4, r], tok_sem.at[1, j], sib)
        normalize(ys4, r.start, r.stop - r.start)
        recv(xraw.at[yo4, r], tok_sem.at[1, j], sib)
        normalize(yo4, r.start, r.stop - r.start)

    def project(t, yy, lo, hi):
        n = hi - lo
        a = xn[pl.ds(2 * yy, 2), lo:hi, :].reshape(2 * n, width)
        w = jnp.concatenate(
            [jnp.concatenate([wbuf[2 * t + i, h, zz, yc // 2, yc % 2] for i in range(2)], axis=1)
             for zz in range(nz) for yc in range(4) for h in range(2)], axis=0)
        r = jnp.dot(a, w, preferred_element_type=jnp.float32).astype(jnp.bfloat16)
        for i in range(2):
            part = r[i * n:(i + 1) * n]
            if t == 0:
                win[REACH + 2 * yy + i, lo:hi, :] = part
            else:
                for h in range(2):
                    qbuf[t - 1, 2 * yy + i, lo // HD, h] = part[:, h * HD:(h + 1) * HD]

    def halo_send(yy, ch):
        r = slice(*cuts[ch:ch + 2])
        for slot in range(4):
            mine = (slot // 2) == yy
            a = win.at[REACH + slot, r]
            if slot > 0:
                send(S_UP, a, win.at[slot - 1, r], halo_sem.at[0], zp, mine & has_zp)
            if slot < 3:
                send(S_DOWN, a, win.at[REACH + 4 + slot, r], halo_sem.at[1], zm, mine & has_zm)

    def halo_recv():
        recv(win.at[0:REACH], halo_sem.at[0], zm, has_zm)
        recv(win.at[REACH + 4:SLOTS], halo_sem.at[1], zp, has_zp)

    def ids_send():
        recv(idwin.at[0:3 * NCH], id_sem.at[0], sib)
        edge = NCH * REACH
        a = NCH * (REACH + 4)
        send(S_IDUP, idwin.at[a - edge:a], idwin.at[0:edge], id_sem.at[1], zp, has_zp)
        send(S_IDDOWN, idwin.at[edge:2 * edge], idwin.at[a:a + edge], id_sem.at[2], zm, has_zm)

    def ids_recv():
        edge = NCH * REACH
        a = NCH * (REACH + 4)
        recv(idwin.at[0:edge], id_sem.at[1], zm, has_zm)
        recv(idwin.at[a:a + edge], id_sem.at[2], zp, has_zp)
        lane = lax.broadcasted_iota(jnp.int32, (8, HD), 1)
        ids = jnp.zeros((8, HD), jnp.int32)
        for j in range(SLOTS * NCH):
            ids = jnp.where(lane == j, idwin[j], ids)
        for j in range(edge, a):
            opening = jnp.min(jnp.where(ids == idwin[j], lane, j))
            starts[j - edge] = jnp.maximum(opening, j - edge)

    rate = HD ** (-0.5) * math.log2(math.e)
    span = REACH * NCH + 1

    def attend(slot, t):
        kv = win.reshape(SLOTS * NCH, HD, SW)
        for qb in range(NCH):
            mine = idwin[NCH * (REACH + slot) + qb, 0:1, :]
            start = starts[NCH * slot + qb]
            bias = jnp.concatenate(
                [jnp.where(idwin[start + j, 0:1, :] == mine, 0.0, -1e30) for j in range(span)], axis=1)
            q = qbuf[t, slot, qb].reshape(2 * HD, HD)
            at = pl.ds(start, span)
            k = kv[at, :, 0:HD].reshape(span * HD, HD)
            v = jnp.concatenate([kv[at, :, HD:SW].reshape(span * HD, HD),
                                 jnp.ones((span * HD, HD), jnp.bfloat16)], axis=1)
            sc = lax.dot_general(q, k, (((1,), (1,)), ((), ())), preferred_element_type=jnp.float32) + bias
            top = jnp.max(sc, axis=-1, keepdims=True)
            w = jnp.exp2((sc - top) * rate).astype(jnp.bfloat16)
            o = jnp.dot(w, v, preferred_element_type=jnp.float32)
            o = (o[:, 0:HD] / o[:, HD:SW]).astype(jnp.bfloat16)
            rr = slice(qb * HD, (qb + 1) * HD)
            obuf[t, slot, rr, 0:HD] = o[0:HD]
            obuf[t, slot, rr, HD:SW] = o[HD:SW]

    def out_cols(head, t):
        return out_ref.at[:, pl.ds(pl.multiple_of(head * (GQ * HD) + t * SW, HD), SW)]

    def attend_slots(t, group):
        for i, slot, dev in group:
            attend(slot, t)
            src = obuf.at[t, slot]
            if dev is None:
                local(src, out_cols(me4, t), 2)
            else:
                send(S_OUT, src, out_cols(me4, t), out_sem, dev)

    last = nz - 1
    held = ((5, last - 1), (4, last), (5, last))
    order = sorted(((t, d) for t in range(SETS) for d in range(nz) if (t, d) not in held),
                   key=lambda td: (nz - 1) * td[0] + (nz - 0.5) * td[1])
    after = {}

    def at_task(index, f):
        after.setdefault(min(index, len(order) - 1), []).append(f)

    def kv_early():
        finish(0)
        project(0, y, 0, HD)
        project(0, y, HD, rows)
        project(0, 1 - y, 0, HD)
        halo_send(1 - y, 0)

    def kv_more():
        tokens(2)
        project(0, 1 - y, *cuts[1:3])
        halo_send(1 - y, 1)
        for ch in range(CHUNKS):
            halo_send(y, ch)

    def own_tokens():
        loc_x.wait()
        loc_in[4].wait()
        normalize(me4)

    def sib_tokens():
        recv(xraw.at[sib4], tok_sem.at[2, 0], sib)
        normalize(sib4)
        pl.when(z < 1)(blank(0))
        pl.when(z + 1 >= nz)(blank(REACH + 4))

    at_task(order.index((2, 0)), own_tokens)
    at_task(order.index((3, 0)), ids_send)
    at_task(order.index((3, 0)), sib_tokens)
    at_task(order.index((0, last)), lambda: tokens(0))
    at_task(order.index((4, 1)), lambda: tokens(1))
    at_task(order.index((1, last)) + 2, kv_early)
    at_task(max(order.index((4, min(2, last))), order.index((1, last)) + 3), kv_more)
    gathered = 0
    for i, (t, d) in enumerate(order):
        while gathered < SETS and (gathered <= t or d > 0 or gathered <= i + 1):
            gather(gathered)
            gathered += 1
        relay(t, d)
        for f in after.get(i, ()):
            f()
    tokens(3)
    tokens(4)
    project(0, 1 - y, *cuts[2:4])
    halo_send(1 - y, 2)
    relay(*held[0])
    relay(*held[1])
    finish(1)
    for yy in (1 - y, y):
        project(1, yy, 0, HD)
        project(1, yy, HD, rows)
    ids_recv()
    halo_recv()
    far = ((0, yo4, yother), (1, ys4, ysame))
    near = ((2, sib4, sib), (3, me4, None))
    attend_slots(0, far)
    relay(*held[2])
    attend_slots(0, near)
    finish(2)
    project(2, 1 - y, 0, HD)
    project(2, 1 - y, HD, rows)
    attend_slots(1, far)
    project(2, y, 0, HD)
    project(2, y, HD, rows)
    attend_slots(1, near)
    recv(obuf.at[:, 0:3], out_sem, sib)
    pltpu.make_async_copy(obuf.at[:, 0], obuf.at[:, 0], loc_sem.at[2]).wait()
    sent(S_MATE, wbuf.at[:, 0, 0, 0])
    sent(S_LATE, wbuf.at[0:len(LATE), 0, 0, 0])
    sent(S_XMATE, wbuf.at[0:SETS - len(LATE), 0, 0, 0])
    sent(S_SIB, wbuf.at[:, :, 0, 0, 0])
    sent(S_IDS, idwin.at[0:3 * NCH])
    sent(S_IDUP, idwin.at[0:NCH * REACH], has_zp)
    sent(S_IDDOWN, idwin.at[0:NCH * REACH], has_zm)
    sent(S_TOK, xraw.at[0:3])
    sent(S_UP, win.at[0:REACH], has_zp)
    sent(S_DOWN, win.at[0:REACH], has_zm)
    sent(S_OUT, obuf.at[:, 0:3])
    sent(S_X, wbuf.at[:, 0, 0:nz - 1])
    for d in range(nz - 1):
        sent(S_Z + 2 * d, wbuf.at[:, 0, 0], has_zp & (z >= d))
        sent(S_Z + 2 * d + 1, wbuf.at[:, 0, 0], has_zm & (z + d < nz))


def solution(mesh):
    n_seq = mesh.shape["seq"]
    n_chips = n_seq // 2
    nz = n_chips // 2

    def on_device(tokens, norm_gain, w_query, w_key, w_value, passage_blocks):
        rows, width = tokens.shape
        anywhere = pl.BlockSpec(memory_space=pl.ANY)
        hbm = pl.BlockSpec(memory_space=pltpu.HBM)
        bf = jnp.bfloat16
        dma = pltpu.SemaphoreType.DMA
        half = w_query.shape[0] // 2
        halves = [w.reshape(2, half, w.shape[1]) for w in (w_query, w_key, w_value)]
        return pl.pallas_call(
            functools.partial(kernel, n_chips),
            out_shape=jax.ShapeDtypeStruct((rows, QH * HD), bf),
            in_specs=[hbm] * 6,
            out_specs=anywhere,
            scratch_shapes=[
                pltpu.VMEM((1, width), jnp.float32),
                pltpu.SMEM(passage_blocks.shape, jnp.int32),
                pltpu.SMEM((4 * NCH,), jnp.int32),
                pltpu.VMEM((4, rows, width), bf),
                pltpu.VMEM((4, rows, width), bf),
                *(pltpu.VMEM((2, half, w.shape[1]), bf) for w in (w_key, w_value, w_query)),
                pltpu.VMEM((SETS, 2, nz, 2, 2, half, HD), bf),
                pltpu.VMEM((2, 4, NCH, 2, HD, HD), bf),
                pltpu.VMEM((SLOTS, rows, SW), bf),
                pltpu.VMEM((SLOTS * NCH, 8, HD), jnp.int32),
                pltpu.VMEM((2, 4, rows, SW), bf),
                dma((S_Z + 2 * (nz - 1),)), dma((8,)), dma((1 + SETS,)), dma, dma((2,)),
                dma((sum(SPLIT) * 2 * (nz - 1),)), dma((3,)), dma((3, len(PIECES) - 1)), dma((3,)), dma((2,)), dma,
            ],
            compiler_params=pltpu.CompilerParams(
                collective_id=0, has_side_effects=True, vmem_limit_bytes=52 * 2**20),
        )(*(pltpu.with_memory_space_constraint(a, pltpu.HBM)
            for a in (tokens, norm_gain[None, :], *halves, passage_blocks)))

    in_specs = (
        P(("groups", "seq"), None),
        P(),
        P("seq", None),
        P("seq", None),
        P("seq", None),
        P(("groups", "seq")),
    )
    out_specs = P(("groups", "seq"), None)
    return jax.shard_map(on_device, mesh=mesh, in_specs=in_specs, out_specs=out_specs, check_vma=False)
```

time: 91.1 us -> 86.7 us (0.952)
  Pallas kernels: 89.4 us -> 85.5 us
    pallas_call x1, Pallas kernels: 89.4 us -> 85.5 us  [on_device(): pl.pallas_call(functools.partial(kernel, n_chips), out_shape=jax.ShapeDty...]
where the time goes in v3:
time: 86.7 us; the launch traced here: 86.5 us
  Pallas kernels  85.5 us (99%)
  local copies, waits for them, and re-layouts  0.97 us (1%)
    pallas_call x1, Pallas kernels, on_device(): pl.pallas_call(functools.partial(kernel, n_chips), out_shape=jax.ShapeDty...  85.5 us

profile of v3, /device:TPU:0, one launch (start us, length us, event | category | flops | bytes accessed | tf_op | source)
XLA Modules:
  0.0 86.5 jit_solution(10911233950252413921)
XLA Ops:
  0.0 85.5 %shard_map.64 = bf16[256,2048]{1,0:T(8,128)(2,1)S(1)} custom-call(bf16[256,4096]{1,0:T(8,128)(2,1)} %tok_ref.1, f32[1,4096]{1,0:T(1,128)} %bitcast.7, bf16[2,128,2048]{2,1,0:T(8,128)(2,1)} %bitcast.4, bf16[2,128,512]{2,1,0:T(8,128)(2,1)} %bitcast.5, bf16[2,128,512]{2,1,0:T(8,128)(2,1)} %bitcast.6, s32[2]{0:T(128)} %id_ref.1), custom_call_target="tpu_custom_call" | custom-call | tf_op jit(solution)/shard_map/pallas_call | solution.py:402
  85.5 1.0 %copy.8 = bf16[256,2048]{1,0:T(8,128)(2,1)} copy(bf16[256,2048]{1,0:T(8,128)(2,1)S(1)} %shard_map.64) | data formatting | bytes 2097152

commit v4 on v3

--- a/solution.py
+++ b/solution.py
@@ -16,12 +16,11 @@
 MESH = pl.DeviceIdType.MESH
 SETS = 2 + GQ
 SW = 2 * HD
-PIECES = (0, 4, 8, 12, 14, 16)
+PIECES = (0, 4, 8, 12, 14, 15, 16)
 SLOTS = 2 * REACH + 4
 NCH = 2
 LATE = (4, 5)
 SPLIT = (2, 1, 1, 1, 1, 4)
-CHUNKS = 3
 (S_MATE, S_LATE, S_XMATE, S_SIB, S_IDS, S_IDUP, S_IDDOWN, S_TOK, S_UP, S_DOWN, S_OUT, S_X, S_Z) = range(13)
 
 
@@ -109,7 +108,7 @@
     pl.semaphore_wait(barrier, 4 + jnp.where(has_zm, 1, 0) + jnp.where(has_zp, 1, 0))
 
     pcuts = [rows * q // 16 for q in PIECES]
-    cuts = (0, rows // 2, rows // 4 * 3, rows)
+    half, quarter, eighth = rows // 2, rows // 4 * 3, rows // 8 * 7
     for i in range(SETS):
         if i < 3:
             loc_in[i].wait()
@@ -150,7 +149,8 @@
     zkeys = {}
 
     def z_at(*key):
-        return zsem.at[zkeys.setdefault(key, len(zkeys))]
+        t, way, d, k = key
+        return zsem.at[zkeys.setdefault((t, way if 2 * d < nz else 0, d, k), len(zkeys))]
 
     def gather(t):
         if t == 0:
@@ -224,8 +224,8 @@
                 for h in range(2):
                     qbuf[t - 1, 2 * yy + i, lo // HD, h] = part[:, h * HD:(h + 1) * HD]
 
-    def halo_send(yy, ch):
-        r = slice(*cuts[ch:ch + 2])
+    def halo_send(yy, lo, hi):
+        r = slice(lo, hi)
         for slot in range(4):
             mine = (slot // 2) == yy
             a = win.at[REACH + slot, r]
@@ -308,14 +308,13 @@
         project(0, y, 0, HD)
         project(0, y, HD, rows)
         project(0, 1 - y, 0, HD)
-        halo_send(1 - y, 0)
+        halo_send(1 - y, 0, half)
 
     def kv_more():
         tokens(2)
-        project(0, 1 - y, *cuts[1:3])
-        halo_send(1 - y, 1)
-        for ch in range(CHUNKS):
-            halo_send(y, ch)
+        project(0, 1 - y, half, quarter)
+        halo_send(1 - y, half, quarter)
+        halo_send(y, 0, rows)
 
     def own_tokens():
         loc_x.wait()
@@ -335,18 +334,22 @@
     at_task(order.index((4, 1)), lambda: tokens(1))
     at_task(order.index((1, last)) + 2, kv_early)
     at_task(max(order.index((4, min(2, last))), order.index((1, last)) + 3), kv_more)
-    gathered = 0
+    gathered = moved = 0
     for i, (t, d) in enumerate(order):
-        while gathered < SETS and (gathered <= t or d > 0 or gathered <= i + 1):
+        moved += d > 0
+        while gathered < SETS and gathered <= max(t, moved + 1 if moved else 0):
             gather(gathered)
             gathered += 1
         relay(t, d)
         for f in after.get(i, ()):
             f()
     tokens(3)
+    project(0, 1 - y, quarter, eighth)
+    halo_send(1 - y, quarter, eighth)
     tokens(4)
-    project(0, 1 - y, *cuts[2:4])
-    halo_send(1 - y, 2)
+    tokens(5)
+    project(0, 1 - y, eighth, rows)
+    halo_send(1 - y, eighth, rows)
     relay(*held[0])
     relay(*held[1])
     finish(1)
@@ -417,7 +420,7 @@
                 pltpu.VMEM((SLOTS * NCH, 8, HD), jnp.int32),
                 pltpu.VMEM((2, 4, rows, SW), bf),
                 dma((S_Z + 2 * (nz - 1),)), dma((8,)), dma((1 + SETS,)), dma, dma((2,)),
-                dma((sum(SPLIT) * 2 * (nz - 1),)), dma((3,)), dma((3, len(PIECES) - 1)), dma((3,)), dma((2,)), dma,
+                dma((sum(SPLIT) * sum(2 if 2 * d < nz else 1 for d in range(1, nz)),)), dma((3,)), dma((3, len(PIECES) - 1)), dma((3,)), dma((2,)), dma,
             ],
             compiler_params=pltpu.CompilerParams(
                 collective_id=0, has_side_effects=True, vmem_limit_bytes=52 * 2**20),

time: 86.7 us -> 84.1 us (0.970)
  Pallas kernels: 85.5 us -> 82.9 us
    pallas_call x1, Pallas kernels: 85.5 us -> 82.9 us  [on_device(): pl.pallas_call(functools.partial(kernel, n_chips), out_shape=jax.ShapeDty...]
where the time goes in v4:
time: 84.1 us; the launch traced here: 83.9 us
  Pallas kernels  82.9 us (99%)
  local copies, waits for them, and re-layouts  0.97 us (1%)
    pallas_call x1, Pallas kernels, on_device(): pl.pallas_call(functools.partial(kernel, n_chips), out_shape=jax.ShapeDty...  82.9 us

profile of v4, /device:TPU:0, one launch (start us, length us, event | category | flops | bytes accessed | tf_op | source)
XLA Modules:
  0.0 83.9 jit_solution(8436424782946381226)
XLA Ops:
  0.0 82.9 %shard_map.64 = bf16[256,2048]{1,0:T(8,128)(2,1)S(1)} custom-call(bf16[256,4096]{1,0:T(8,128)(2,1)} %tok_ref.1, f32[1,4096]{1,0:T(1,128)} %bitcast.7, bf16[2,128,2048]{2,1,0:T(8,128)(2,1)} %bitcast.4, bf16[2,128,512]{2,1,0:T(8,128)(2,1)} %bitcast.5, bf16[2,128,512]{2,1,0:T(8,128)(2,1)} %bitcast.6, s32[2]{0:T(128)} %id_ref.1), custom_call_target="tpu_custom_call" | custom-call | tf_op jit(solution)/shard_map/pallas_call | solution.py:405
  82.9 1.0 %copy.8 = bf16[256,2048]{1,0:T(8,128)(2,1)} copy(bf16[256,2048]{1,0:T(8,128)(2,1)S(1)} %shard_map.64) | data formatting | bytes 2097152

commit v5 on v4

--- a/solution.py
+++ b/solution.py
@@ -209,20 +209,25 @@
         recv(xraw.at[yo4, r], tok_sem.at[1, j], sib)
         normalize(yo4, r.start, r.stop - r.start)
 
-    def project(t, yy, lo, hi):
-        n = hi - lo
-        a = xn[pl.ds(2 * yy, 2), lo:hi, :].reshape(2 * n, width)
+    def product(t, a):
         w = jnp.concatenate(
             [jnp.concatenate([wbuf[2 * t + i, h, zz, yc // 2, yc % 2] for i in range(2)], axis=1)
              for zz in range(nz) for yc in range(4) for h in range(2)], axis=0)
-        r = jnp.dot(a, w, preferred_element_type=jnp.float32).astype(jnp.bfloat16)
+        return jnp.dot(a, w, preferred_element_type=jnp.float32).astype(jnp.bfloat16)
+
+    def project(yy, lo, hi):
+        n = hi - lo
+        r = product(0, xn[pl.ds(2 * yy, 2), lo:hi, :].reshape(2 * n, width))
         for i in range(2):
-            part = r[i * n:(i + 1) * n]
-            if t == 0:
-                win[REACH + 2 * yy + i, lo:hi, :] = part
-            else:
+            win[REACH + 2 * yy + i, lo:hi, :] = r[i * n:(i + 1) * n]
+
+    def queries2(t, yy):
+        r = product(t, xn[pl.ds(2 * yy, 2)].reshape(2 * rows, width))
+        for i in range(2):
+            for qb in range(NCH):
                 for h in range(2):
-                    qbuf[t - 1, 2 * yy + i, lo // HD, h] = part[:, h * HD:(h + 1) * HD]
+                    lo = i * rows + qb * HD
+                    qbuf[t - 1, 2 * yy + i, qb, h] = r[lo:lo + HD, h * HD:(h + 1) * HD]
 
     def halo_send(yy, lo, hi):
         r = slice(lo, hi)
@@ -285,14 +290,21 @@
     def out_cols(head, t):
         return out_ref.at[:, pl.ds(pl.multiple_of(head * (GQ * HD) + t * SW, HD), SW)]
 
-    def attend_slots(t, group):
-        for i, slot, dev in group:
-            attend(slot, t)
-            src = obuf.at[t, slot]
-            if dev is None:
-                local(src, out_cols(me4, t), 2)
-            else:
-                send(S_OUT, src, out_cols(me4, t), out_sem, dev)
+    def start_local(src, dst):
+        local(src, dst, 2)
+
+    def attend_slot(t, slot):
+        attend(slot, t)
+        src = obuf.at[t, slot]
+        pl.when(slot != me4)(lambda: send(S_OUT, src, out_cols(me4, t), out_sem, (g, 4 * z + slot)))
+        pl.when(slot == me4)(lambda: start_local(src, out_cols(me4, t)))
+
+    def over(first, stop, f):
+        def body(i, _):
+            f(2 * lax.rem(1 - y + i // 2, 2) + lax.rem(1 - c + i, 2))
+            return 0
+
+        lax.fori_loop(first, stop, body, 0)
 
     last = nz - 1
     held = ((5, last - 1), (4, last), (5, last))
@@ -305,14 +317,13 @@
 
     def kv_early():
         finish(0)
-        project(0, y, 0, HD)
-        project(0, y, HD, rows)
-        project(0, 1 - y, 0, HD)
+        project(y, 0, rows)
+        project(1 - y, 0, HD)
         halo_send(1 - y, 0, half)
 
     def kv_more():
         tokens(2)
-        project(0, 1 - y, half, quarter)
+        project(1 - y, half, quarter)
         halo_send(1 - y, half, quarter)
         halo_send(y, 0, rows)
 
@@ -344,32 +355,34 @@
         for f in after.get(i, ()):
             f()
     tokens(3)
-    project(0, 1 - y, quarter, eighth)
+    project(1 - y, quarter, eighth)
     halo_send(1 - y, quarter, eighth)
     tokens(4)
     tokens(5)
-    project(0, 1 - y, eighth, rows)
+    project(1 - y, eighth, rows)
     halo_send(1 - y, eighth, rows)
     relay(*held[0])
     relay(*held[1])
     finish(1)
-    for yy in (1 - y, y):
-        project(1, yy, 0, HD)
-        project(1, yy, HD, rows)
+    queries2(1, 1 - y)
+    queries2(1, y)
     ids_recv()
     halo_recv()
-    far = ((0, yo4, yother), (1, ys4, ysame))
-    near = ((2, sib4, sib), (3, me4, None))
-    attend_slots(0, far)
+    over(0, 2, lambda slot: attend_slot(0, slot))
     relay(*held[2])
-    attend_slots(0, near)
+
+    def near(slot):
+        attend_slot(0, slot)
+
+    def late(slot):
+        attend_slot(1, slot)
+
+    over(2, 4, near)
     finish(2)
-    project(2, 1 - y, 0, HD)
-    project(2, 1 - y, HD, rows)
-    attend_slots(1, far)
-    project(2, y, 0, HD)
-    project(2, y, HD, rows)
-    attend_slots(1, near)
+    queries2(2, 1 - y)
+    over(0, 2, late)
+    queries2(2, y)
+    over(2, 4, late)
     recv(obuf.at[:, 0:3], out_sem, sib)
     pltpu.make_async_copy(obuf.at[:, 0], obuf.at[:, 0], loc_sem.at[2]).wait()
     sent(S_MATE, wbuf.at[:, 0, 0, 0])

time: 84.1 us -> 83.8 us (level)
  no operation moved by 1% of the time
where the time goes in v5:
time: 83.8 us; the launch traced here: 83.6 us
  Pallas kernels  82.6 us (99%)
  local copies, waits for them, and re-layouts  0.97 us (1%)
    pallas_call x1, Pallas kernels, on_device(): pl.pallas_call(functools.partial(kernel, n_chips), out_shape=jax.ShapeDty...  82.6 us

profile of v5, /device:TPU:0, one launch (start us, length us, event | category | flops | bytes accessed | tf_op | source)
XLA Modules:
  0.0 83.6 jit_solution(2632179787509070570)
XLA Ops:
  0.0 82.6 %shard_map.64 = bf16[256,2048]{1,0:T(8,128)(2,1)S(1)} custom-call(bf16[256,4096]{1,0:T(8,128)(2,1)} %tok_ref.1, f32[1,4096]{1,0:T(1,128)} %bitcast.7, bf16[2,128,2048]{2,1,0:T(8,128)(2,1)} %bitcast.4, bf16[2,128,512]{2,1,0:T(8,128)(2,1)} %bitcast.5, bf16[2,128,512]{2,1,0:T(8,128)(2,1)} %bitcast.6, s32[2]{0:T(128)} %id_ref.1), custom_call_target="tpu_custom_call" | custom-call | tf_op jit(solution)/shard_map/pallas_call | solution.py:418
  82.6 1.0 %copy.8 = bf16[256,2048]{1,0:T(8,128)(2,1)} copy(bf16[256,2048]{1,0:T(8,128)(2,1)S(1)} %shard_map.64) | data formatting | bytes 2097152
